TPU v7x, 128 devices: a whole 4x4x4 slice. The times are simulated.
128 devices in a mesh: req: 64 (over z, y, x), kv: 2 (over core).
Axes of the slice: x: 4, y: 4, z: 4, core: 2. Of those that a mesh axis runs over, the one named last changes fastest.
Arguments:
- queries: bfloat16 [16384, 2048], P(('req', 'kv')), may hold values from -6 to 6
- keys: bfloat16 [16384, 1024], P(('req', 'kv')), may hold values from -6 to 6
- values: bfloat16 [16384, 1024], P(('req', 'kv')), may hold values from -6 to 6
- residual: bfloat16 [16384, 3584], P(('req', 'kv'))
- segment_ids: int32 [16384], P(('req', 'kv')), may hold values from 127 to 16383, as said below
- regroup: int32 [16384], P(('req', 'kv')), may hold values from 0 to 16383, as said below
- out_weight: bfloat16 [2048, 3584], P('kv')
- attn_gain: float32 [3584], replicated, may hold values from 0.1 to 1.9
- pre_gain: float32 [3584], replicated, may hold values from 0.1 to 1.9
- gate_weight: bfloat16 [3584, 7168], P(None, 'kv'), may hold values from -0.09375 to 0.09375
- up_weight: bfloat16 [3584, 7168], P(None, 'kv'), may hold values from -0.09375 to 0.09375
- down_weight: bfloat16 [7168, 3584], P('kv')
- post_gain: float32 [3584], replicated, may hold values from 0.1 to 1.9
Outputs:
- layer_out: bfloat16 [16384, 3584], P(('req', 'kv'))
- key_cache_rows: bfloat16 [4, 16384, 256], P(None, ('req', 'kv'))
- value_cache_rows: bfloat16 [4, 16384, 256], P(None, ('req', 'kv'))
Inputs may be any that keep to these rules, and one draw needn't show every extreme that they name: `segment_ids`: A request is a run of consecutive slots carrying one id, the index of its last slot; no request runs from one index of req's 256 slots into the next. `regroup`: A permutation of the slots. Each device (in req+kv order) sends exactly one of its 128 slots to each of the 128 devices: for every pair of devices, exactly one slot of the first has its output row among the 128 rows of the second.
All inputs are finite; a program needn't handle non-finite values.
Results may differ from a plain program's by a relative error of at most 0.0095.
Values may be sent and summed in bfloat16 or wider, within the bound.
A program may use at most 192 MiB of HBM per device.

v0:
```python
import jax
import jax.numpy as jnp
from jax import lax
from jax.sharding import PartitionSpec as P

QUERY_HEADS = 8
KEY_VALUE_HEADS = 4
HEAD_ENTRIES = 256
WINDOW_REACH = 512
cap_value = 50.0
norm_eps = 1e-06


def from_behind(block, axis, distance):
    devices = range(lax.axis_size(axis))
    route = [(i - distance, i) for i in devices if i - distance in devices]
    return lax.ppermute(block, axis, route)


def rms_scale(values_in, gain_row):
    mean_square = jnp.mean(values_in * values_in, axis=-1, keepdims=True)
    return values_in * lax.rsqrt(mean_square + norm_eps) * gain_row


def key_mask(own_ids, key_ids, key_pos):
    distance = jnp.arange(own_ids.shape[0], dtype=jnp.int32)[:, None] - key_pos[None, :]
    return (own_ids[:, None] == key_ids[None, :]) & (distance >= 0) & (distance < WINDOW_REACH)


def block_terms(query_head_rows, key_heads, value_heads, allowed):
    raw_scores = jnp.einsum(
        "tkgd,skd->kgts", query_head_rows, key_heads, preferred_element_type=jnp.float32
    )
    scores = cap_value * jnp.tanh(raw_scores * HEAD_ENTRIES ** (-0.5) / cap_value)
    weights = jnp.where(allowed, jnp.exp(scores), 0.0)
    totals = jnp.sum(weights, axis=-1)
    numerator = jnp.einsum(
        "kgts,skd->tkgd",
        weights.astype(jnp.bfloat16),
        value_heads,
        preferred_element_type=jnp.float32,
    )
    return (numerator, totals)


def send_rows(normed_part, normed_pos, stream_part, key_portion, value_portion):
    received = (
        lax.all_to_all(normed_part, ("req", "kv"), split_axis=0, concat_axis=0, tiled=True),
        lax.all_to_all(normed_pos, ("req", "kv"), split_axis=0, concat_axis=0, tiled=True),
        lax.all_to_all(stream_part, ("req", "kv"), split_axis=0, concat_axis=0, tiled=True),
        lax.all_to_all(key_portion, ("req", "kv"), split_axis=0, concat_axis=0, tiled=True),
        lax.all_to_all(value_portion, ("req", "kv"), split_axis=0, concat_axis=0, tiled=True),
    )
    return received


def per_device(
    queries,
    keys,
    values,
    residual,
    segment_ids,
    regroup,
    out_weight,
    attn_gain,
    pre_gain,
    gate_weight,
    up_weight,
    down_weight,
    post_gain,
):
    resident_rows = queries.shape[0]
    grouped_heads = QUERY_HEADS // KEY_VALUE_HEADS
    query_head_rows = queries.reshape(resident_rows, KEY_VALUE_HEADS, grouped_heads, HEAD_ENTRIES)
    own_ids = segment_ids + 1
    base_pos = jnp.arange(resident_rows, dtype=jnp.int32)
    key_collections = [(keys, values, own_ids, base_pos)]
    moved_keys, moved_values, moved_ids = from_behind((keys, values, own_ids), "kv", 1)
    key_collections.append((moved_keys, moved_values, moved_ids, base_pos - resident_rows))
    gathered_keys = jnp.concatenate(
        [key_collection[0] for key_collection in key_collections], axis=0
    ).reshape(-1, KEY_VALUE_HEADS, HEAD_ENTRIES)
    gathered_values = jnp.concatenate(
        [key_collection[1] for key_collection in key_collections], axis=0
    ).reshape(-1, KEY_VALUE_HEADS, HEAD_ENTRIES)
    all_ids = jnp.concatenate([key_collection[2] for key_collection in key_collections], axis=0)
    all_pos = jnp.concatenate([key_collection[3] for key_collection in key_collections], axis=0)
    numerator, totals = block_terms(
        query_head_rows, gathered_keys, gathered_values, key_mask(own_ids, all_ids, all_pos)
    )
    attended_output = (
        (numerator / jnp.transpose(totals, (2, 0, 1))[..., None])
        .astype(jnp.bfloat16)
        .reshape(resident_rows, QUERY_HEADS * HEAD_ENTRIES)
    )
    head_rows = lax.all_to_all(attended_output, "kv", split_axis=1, concat_axis=0, tiled=True)
    picked = head_rows
    projected = lax.psum_scatter(
        jnp.dot(picked, out_weight, preferred_element_type=jnp.float32).astype(jnp.bfloat16),
        "kv",
        scatter_dimension=0,
        tiled=True,
    ).astype(jnp.float32)
    stream = (residual.astype(jnp.float32) + rms_scale(projected, attn_gain)).astype(jnp.bfloat16)
    normed = rms_scale(stream.astype(jnp.float32), pre_gain).astype(jnp.bfloat16)
    row_order = jnp.argsort(regroup)
    destination_rows = regroup[row_order]
    sorted_normed = normed[row_order]
    sorted_stream = stream[row_order]
    sorted_keys = keys[row_order]
    sorted_values = values[row_order]
    received = send_rows(
        sorted_normed, destination_rows % resident_rows, sorted_stream, sorted_keys, sorted_values
    )
    placed = jnp.argsort(received[1])
    own_normed = received[0][placed]
    group_normed = lax.all_gather(own_normed, "kv", axis=0, tiled=True)
    own_stream = received[2][placed]
    resident_keys = received[3][placed]
    resident_values = received[4][placed]
    picked = group_normed
    gate_part = jnp.dot(picked, gate_weight, preferred_element_type=jnp.float32)
    up_part = jnp.dot(picked, up_weight, preferred_element_type=jnp.float32)
    active = (jax.nn.gelu(gate_part, approximate=True) * up_part).astype(jnp.bfloat16)
    ffw_sum = lax.psum_scatter(
        jnp.dot(active, down_weight, preferred_element_type=jnp.float32).astype(jnp.bfloat16),
        "kv",
        scatter_dimension=0,
        tiled=True,
    ).astype(jnp.float32)
    layer_out = (own_stream.astype(jnp.float32) + rms_scale(ffw_sum, post_gain)).astype(
        jnp.bfloat16
    )
    key_cache_rows = resident_keys.reshape(resident_rows, KEY_VALUE_HEADS, HEAD_ENTRIES).transpose(
        1, 0, 2
    )
    value_cache_rows = resident_values.reshape(
        resident_rows, KEY_VALUE_HEADS, HEAD_ENTRIES
    ).transpose(1, 0, 2)
    return (layer_out, key_cache_rows, value_cache_rows)


def solution(mesh):
    placed = (
        P(("req", "kv"), None),
        P(("req", "kv"), None),
        P(("req", "kv"), None),
        P(("req", "kv"), None),
        P(("req", "kv")),
        P(("req", "kv")),
        P("kv", None),
        P(),
        P(),
        P(None, "kv"),
        P(None, "kv"),
        P("kv", None),
        P(),
    )
    return jax.shard_map(
        per_device,
        mesh=mesh,
        in_specs=placed,
        out_specs=(
            P(("req", "kv"), None),
            P(None, ("req", "kv"), None),
            P(None, ("req", "kv"), None),
        ),
        check_vma=False,
    )
```

profile of v0, /device:TPU:1, one launch (start us, length us, event | category | flops | bytes accessed | tf_op | source)
XLA Modules:
  0.0 216.2 jit_solution(5172984267959892114)
XLA Ops:
  7.9 1.3 collective-permute-start.1
  9.2 1.1 copy.46
  10.3 1.3 collective-permute-start.2
  11.6 1.3 collective-permute-start
  12.9 1.4 reshape.106
  14.5 1.0 collective-permute-done
  15.5 1.0 pad_maximum_fusion
  17.9 4.2 %all_to_all.76 = bf16[128,2,1024]{2,0,1:T(8,128)(2,1)S(1)} all-to-all(bf16[128,2,1024]{2,0,1:T(8,128)(2,1)S(1)} %copy.50), channel_id=1, replica_groups=mesh['req'=64,'kv'=2] {'kv'}, dimensions={1} | all-to-all | bytes 1048576 | tf_op jit(solution)/shard_map/all_to_all | solution.py:96
  22.1 6.4 %convolution_convert_fusion.1 = bf16[256,3584]{1,0:T(8,128)(2,1)} fusion(bf16[256,1024]{1,0:T(8,128)(2,1)S(1)} %bitcast.76, bf16[1024,3584]{1,0:T(8,128)(2,1)} %param.19), kind=kOutput, calls=%fused_computation.13 | convolution fusion | flops 1879965696 | bytes 9699328 | tf_op jit(solution)/shard_map/dot_general | solution.py:99
  29.2 2.5 %sort.31 = (s32[128]{0:T(128)}, s32[128]{0:T(128)S(1)}) sort(s32[128]{0:T(128)S(1)} %copy-done, s32[128]{0:T(128)S(1)} %iota.18), dimensions={0}, to_apply=%region_3.4 | sort | flops 896 | bytes 2048 | tf_op jit(solution)/shard_map/jit(argsort)/sort | solution.py:106
  31.8 1.2 gather_fusion.1
  33.8 10.9 %all-to-all-start.2 = ((s32[128,1,1]{2,1,0:T(1,128)}), s32[128,1,1]{2,1,0:T(1,128)S(1)}, u32[]{:S(2)}, u32[]{:S(2)}) async-start(s32[128,1,1]{2,1,0:T(1,128)} %copy.52), calls=%async_computation.3 | async-start | bytes 131072 | tf_op jit(solution)/shard_map/all_to_all | solution.py:49
  44.7 1.4 fusion.8
  46.2 1.8 fusion.12
  48.3 1.1 gather_fusion.3
  49.9 1.2 reduce.1
  51.1 1.1 reshape.194
  52.2 2.0 all-to-all-done.2
  54.2 7.8 %all-to-all-start.3 = ((bf16[128,2,1792]{2,1,0:T(2,128)(2,1)}), bf16[128,2,1792]{2,1,0:T(2,128)(2,1)S(1)}, u32[]{:S(2)}, u32[]{:S(2)}) async-start(bf16[128,2,1792]{2,1,0:T(2,128)(2,1)} %reshape.194), calls=%async_computation.4 | async-start | bytes 1835008 | tf_op jit(solution)/shard_map/all_to_all | solution.py:48
  62.0 2.4 %reduce = s32[128]{0:T(128)S(1)} reduce(s32[128,1,1]{2,1,0:T(1,128)S(1)} %all-to-all-done.2, s32[]{:T(128)} %constant.17.clone.1), dimensions={1,2}, to_apply=%all_to_all.59.reduce_sub_computation | reduce | bytes 1028 | tf_op jit(solution)/shard_map/all_to_all | solution.py:49
  64.4 2.5 %sort.32 = (s32[128]{0:T(128)}, s32[128]{0:T(128)S(1)}) sort(s32[128]{0:T(128)S(1)} %reduce, s32[128]{0:T(128)S(1)} %iota.19), dimensions={0}, to_apply=%region_4.5 | sort | flops 896 | bytes 2048 | tf_op jit(solution)/shard_map/jit(argsort)/sort | solution.py:115
  67.0 13.0 %all-to-all-done.3 = bf16[128,2,1792]{2,1,0:T(2,128)(2,1)S(1)} async-done(((bf16[128,2,1792]{2,1,0:T(2,128)(2,1)}), bf16[128,2,1792]{2,1,0:T(2,128)(2,1)S(1)}, u32[]{:S(2)}, u32[]{:S(2)}) %all-to-all-start.3) | async-done | bytes 917536 | tf_op jit(solution)/shard_map/all_to_all | solution.py:48
  79.9 2.1 reshape.195
  82.0 1.6 copy.79
  83.7 2.0 gather_fusion.4
  86.0 9.3 %all-gather.3.cloned.1.call-done = bf16[256,3584]{1,0:T(8,128)(2,1)} async-done(((bf16[128,3584]{1,0:T(8,128)(2,1)}), bf16[256,3584]{1,0:T(8,128)(2,1)}) %all-gather.3.cloned.1.call-update) | async-done | bytes 1835024 | tf_op jit(solution)/shard_map/all_gather | solution.py:117
  95.3 17.1 %fusion.43 = f32[256,3584]{1,0:T(8,128)} fusion(bf16[256,3584]{1,0:T(8,128)(2,1)} %all-gather.3.cloned.1.call-done, bf16[3584,3584]{1,0:T(8,128)(2,1)} %param.22), kind=kOutput, calls=%fused_computation.86 | convolution fusion | flops 6576668672 | bytes 31195136 | tf_op jit(solution)/shard_map/dot_general | solution.py:122
  112.4 24.6 %convolution_convert_fusion = bf16[256,3584]{1,0:T(8,128)(2,1)} fusion(bf16[3584,3584]{1,0:T(8,128)(2,1)} %param.24, bf16[256,3584]{1,0:T(8,128)(2,1)S(1)} %copy-done.7, bf16[3584,3584]{1,0:T(8,128)(2,1)} %param.23, f32[256,3584]{1,0:T(8,128)} %fusion.43), kind=kOutput, calls=%fused_computation.12 | convolution fusion | flops 13163429888 | bytes 58720256 | tf_op jit(solution)/shard_map/dot_general | solution.py:126
  137.0 0.9 copy-done.1
  137.9 0.9 gather_fusion.5
  139.4 0.9 reshape.198
  140.3 9.2 %all-to-all-start.4 = ((bf16[128,2,512]{2,1,0:T(2,128)(2,1)}), bf16[128,2,512]{2,1,0:T(2,128)(2,1)S(1)}, u32[]{:S(2)}, u32[]{:S(2)}) async-start(bf16[128,2,512]{2,1,0:T(2,128)(2,1)} %reshape.198), calls=%async_computation.6 | async-start | bytes 524288 | tf_op jit(solution)/shard_map/all_to_all | solution.py:51
  149.5 0.9 gather_fusion.7
  151.1 0.9 reshape.200
  152.0 8.7 %all-to-all-done.4 = bf16[128,2,512]{2,1,0:T(2,128)(2,1)S(1)} async-done(((bf16[128,2,512]{2,1,0:T(2,128)(2,1)}), bf16[128,2,512]{2,1,0:T(2,128)(2,1)S(1)}, u32[]{:S(2)}, u32[]{:S(2)}) %all-to-all-start.4) | async-done | bytes 262176 | tf_op jit(solution)/shard_map/all_to_all | solution.py:51
  160.6 4.4 %all-to-all-start.5 = ((bf16[128,2,512]{2,1,0:T(2,128)(2,1)}), bf16[128,2,512]{2,1,0:T(2,128)(2,1)S(1)}, u32[]{:S(2)}, u32[]{:S(2)}) async-start(bf16[128,2,512]{2,1,0:T(2,128)(2,1)} %reshape.200), calls=%async_computation.7 | async-start | bytes 524288 | tf_op jit(solution)/shard_map/all_to_all | solution.py:52
  165.0 1.1 gather_fusion
  166.2 1.2 reduce.2
  167.4 1.1 reshape.196
  168.5 7.6 %all-to-all-done.5 = bf16[128,2,512]{2,1,0:T(2,128)(2,1)S(1)} async-done(((bf16[128,2,512]{2,1,0:T(2,128)(2,1)}), bf16[128,2,512]{2,1,0:T(2,128)(2,1)S(1)}, u32[]{:S(2)}, u32[]{:S(2)}) %all-to-all-start.5) | async-done | bytes 262176 | tf_op jit(solution)/shard_map/all_to_all | solution.py:52
  176.1 5.1 %all-to-all-start.1 = ((bf16[128,2,1792]{2,1,0:T(2,128)(2,1)}), bf16[128,2,1792]{2,1,0:T(2,128)(2,1)}, u32[]{:S(2)}, u32[]{:S(2)}) async-start(bf16[128,2,1792]{2,1,0:T(2,128)(2,1)} %reshape.196), calls=%async_computation.2 | async-start | bytes 1835008 | tf_op jit(solution)/shard_map/all_to_all | solution.py:50
  181.6 0.9 gather_fusion.6
  182.8 0.9 gather_fusion.8
  184.5 14.5 %all-to-all-done.1 = bf16[128,2,1792]{2,1,0:T(2,128)(2,1)} async-done(((bf16[128,2,1792]{2,1,0:T(2,128)(2,1)}), bf16[128,2,1792]{2,1,0:T(2,128)(2,1)}, u32[]{:S(2)}, u32[]{:S(2)}) %all-to-all-start.1) | async-done | bytes 917536 | tf_op jit(solution)/shard_map/all_to_all | solution.py:50
  199.0 5.4 %reshape.197 = bf16[128,1,3584]{2,1,0:T(2,128)(2,1)S(1)} reshape(bf16[128,2,1792]{2,1,0:T(2,128)(2,1)} %all-to-all-done.1) | data formatting | bytes 1835008
  204.6 1.1 gather_fusion.2
  205.7 1.4 fusion.15
  207.2 2.5 %fusion.18 = bf16[128,3584]{1,0:T(8,128)(2,1)} fusion(bf16[128,3584]{1,0:T(8,128)(2,1)} %reduce-scatter.5.cloned.1.call-done, bf16[128,3584]{1,0:T(8,128)(2,1)S(1)} %gather_fusion.2, f32[3584]{0:T(1024)S(1)} %copy-done.6, f32[128]{0:T(128)S(1)} %add_rsqrt_fusion), kind=kLoop, calls=%fused_computation.37 | loop fusion | flops 2752512 | bytes 2767360 | tf_op jit(solution)/shard_map/convert_element_type | solution.py:131
  (57 shorter events, 7.7 us)
Async XLA Ops:
  7.2 37.5 %reduce-scatter.3.cloned.1.call-start = ((), (), s32[]{:S(2)}) async-start(), calls=%async_computation.8 | async-start | bytes 2752512 | tf_op jit(solution)/shard_map/reduce_scatter | solution.py:98
  7.9 6.5 %collective-permute-start.1 = (s32[128]{0:T(128)S(1)}, s32[128]{0:T(128)S(1)}, u32[]{:S(2)}, u32[]{:S(2)}) collective-permute-start(s32[128]{0:T(128)S(1)} %broadcast_add_fusion), channel_id=1, source_target_pairs={{0,1},{2,3},{4,5},{6,7},{8,9},{10,11},{12,13},{14,15},{16,17},{18,... | collective-permute-start | bytes 1544 | tf_op jit(solution)/shard_map/ppermute | solution.py:17
  10.3 6.4 %collective-permute-start.2 = (bf16[128,1024]{0,1:T(8,128)(2,1)S(1)}, bf16[128,1024]{0,1:T(8,128)(2,1)S(1)}, u32[]{:S(2)}, u32[]{:S(2)}) collective-permute-start(bf16[128,1024]{0,1:T(8,128)(2,1)S(1)} %copy.46), channel_id=1, source_target_pairs={{0,1},{2,3},{4,5},{6,7},{8,9},{10,11},{12,13},{14,15},{16,17},{18,... | collective-permute-start | bytes 786440 | tf_op jit(solution)/shard_map/ppermute | solution.py:17
  11.6 4.0 %collective-permute-start = (bf16[128,1024]{1,0:T(8,128)(2,1)}, bf16[128,1024]{1,0:T(8,128)(2,1)S(1)}, u32[]{:S(2)}, u32[]{:S(2)}) collective-permute-start(bf16[128,1024]{1,0:T(8,128)(2,1)} %param.15), channel_id=1, source_target_pairs={{0,1},{2,3},{4,5},{6,7},{8,9},{10,11},{12,13},{14,15},{16,17},{18,... | collective-permute-start | bytes 786440 | tf_op jit(solution)/shard_map/ppermute | solution.py:17
  28.6 0.7 copy-start
  28.6 17.6 %copy-start.3 = (bf16[128,3584]{1,0:T(8,128)(2,1)S(1)}, bf16[128,3584]{1,0:T(8,128)(2,1)}, u32[]{:S(2)}) copy-start(bf16[128,3584]{1,0:T(8,128)(2,1)} %param.16) | copy-start | bytes 2752516
  28.6 17.6 %copy-start.4 = (f32[3584]{0:T(1024)S(1)}, f32[3584]{0:T(1024)}, u32[]{:S(2)}) copy-start(f32[3584]{0:T(1024)} %param.20) | copy-start | bytes 43012
  33.8 20.4 %all-to-all-start.2 = ((s32[128,1,1]{2,1,0:T(1,128)}), s32[128,1,1]{2,1,0:T(1,128)S(1)}, u32[]{:S(2)}, u32[]{:S(2)}) async-start(s32[128,1,1]{2,1,0:T(1,128)} %copy.52), calls=%async_computation.3 | async-start | bytes 131072 | tf_op jit(solution)/shard_map/all_to_all | solution.py:49
  44.7 3.3 %copy-start.5 = (f32[3584]{0:T(1024)S(1)}, f32[3584]{0:T(1024)}, u32[]{:S(2)}) copy-start(f32[3584]{0:T(1024)} %param.21) | copy-start | bytes 43012
  54.2 25.8 %all-to-all-start.3 = ((bf16[128,2,1792]{2,1,0:T(2,128)(2,1)}), bf16[128,2,1792]{2,1,0:T(2,128)(2,1)S(1)}, u32[]{:S(2)}, u32[]{:S(2)}) async-start(bf16[128,2,1792]{2,1,0:T(2,128)(2,1)} %reshape.194), calls=%async_computation.4 | async-start | bytes 1835008 | tf_op jit(solution)/shard_map/all_to_all | solution.py:48
  62.0 33.3 %all-gather.3.cloned.1.call-start = ((), (), s32[]{:S(2)}) async-start(), calls=%async_computation.10 | async-start | bytes 2752512 | tf_op jit(solution)/shard_map/all_gather | solution.py:117
  85.7 120.0 %reduce-scatter.5.cloned.1.call-start = ((), (), s32[]{:S(2)}) async-start(), calls=%async_computation.9 | async-start | bytes 2752512 | tf_op jit(solution)/shard_map/reduce_scatter | solution.py:125
  95.3 17.1 %copy-start.7 = (bf16[256,3584]{1,0:T(8,128)(2,1)S(1)}, bf16[256,3584]{1,0:T(8,128)(2,1)}, u32[]{:S(2)}) copy-start(bf16[256,3584]{1,0:T(8,128)(2,1)} %all-gather.3.cloned.1.call-done) | copy-start | bytes 5505028
  136.9 0.9 copy-start.1
  137.9 11.6 %copy-start.2 = (bf16[128,1024]{1,0:T(8,128)(2,1)S(1)}, bf16[128,1024]{1,0:T(8,128)(2,1)}, u32[]{:S(2)}) copy-start(bf16[128,1024]{1,0:T(8,128)(2,1)} %param.15) | copy-start | bytes 786436
  140.3 20.3 %all-to-all-start.4 = ((bf16[128,2,512]{2,1,0:T(2,128)(2,1)}), bf16[128,2,512]{2,1,0:T(2,128)(2,1)S(1)}, u32[]{:S(2)}, u32[]{:S(2)}) async-start(bf16[128,2,512]{2,1,0:T(2,128)(2,1)} %reshape.198), calls=%async_computation.6 | async-start | bytes 524288 | tf_op jit(solution)/shard_map/all_to_all | solution.py:51
  160.6 15.5 %all-to-all-start.5 = ((bf16[128,2,512]{2,1,0:T(2,128)(2,1)}), bf16[128,2,512]{2,1,0:T(2,128)(2,1)S(1)}, u32[]{:S(2)}, u32[]{:S(2)}) async-start(bf16[128,2,512]{2,1,0:T(2,128)(2,1)} %reshape.200), calls=%async_computation.7 | async-start | bytes 524288 | tf_op jit(solution)/shard_map/all_to_all | solution.py:52
  176.1 22.9 %all-to-all-start.1 = ((bf16[128,2,1792]{2,1,0:T(2,128)(2,1)}), bf16[128,2,1792]{2,1,0:T(2,128)(2,1)}, u32[]{:S(2)}, u32[]{:S(2)}) async-start(bf16[128,2,1792]{2,1,0:T(2,128)(2,1)} %reshape.196), calls=%async_computation.2 | async-start | bytes 1835008 | tf_op jit(solution)/shard_map/all_to_all | solution.py:50
  204.6 2.6 %copy-start.6 = (f32[3584]{0:T(1024)S(1)}, f32[3584]{0:T(1024)}, u32[]{:S(2)}) copy-start(f32[3584]{0:T(1024)} %param.25) | copy-start | bytes 43012
Sparse Core Ops, SparseCore 0:
  28.7 15.0 reduce-scatter.2
  85.9 9.4 all-gather.2
  137.1 13.3 reduce-scatter.4
where the time goes:
time: 217 us; the launch traced here: 216 us
  waiting for transfers between devices  56.2 us (26%)
  matrix products  48.9 us (23%)
  starting transfers between devices  41.6 us (19%)
  local copies, waits for them, and re-layouts  30.5 us (14%)
  other arithmetic  20.6 us (9%)
  between operations  14.1 us (6%)
  blocking collectives  4.22 us (2%)
    dot_general x1, matrix products, per_device(): jnp.dot(active, down_weight, preferred_element_type=jnp.float32)  24.6 us
    dot_general x1, matrix products, per_device(): gate_part = jnp.dot(picked, gate_weight, preferred_element_type=jnp.float32)  17.1 us
    unnamed x29, local copies, waits for them, and re-layouts  16.6 us
    all_to_all x1, waiting for transfers between devices, send_rows(): lax.all_to_all(stream_part, ('req', 'kv'), split_axis=0, concat_axis=0, t...  14.5 us
    all_to_all x1, waiting for transfers between devices, send_rows(): lax.all_to_all(normed_part, ('req', 'kv'), split_axis=0, concat_axis=0, t...  13 us
    all_to_all x1, starting transfers between devices, send_rows(): lax.all_to_all(normed_pos, ('req', 'kv'), split_axis=0, concat_axis=0, ti...  10.9 us
    all_gather x1, waiting for transfers between devices, per_device(): group_normed = lax.all_gather(own_normed, 'kv', axis=0, tiled=True)  9.35 us
    all_to_all x1, starting transfers between devices, send_rows(): lax.all_to_all(key_portion, ('req', 'kv'), split_axis=0, concat_axis=0, t...  9.19 us
  transfers between devices with their start and end apart: 11, of which 7 were waited for; matrix products, arithmetic and copies ran while one was open for 18% of the time, Pallas kernels for 0%

commit v1 on v0

--- a/solution.py
+++ b/solution.py
@@ -9,6 +9,11 @@
 WINDOW_REACH = 512
 cap_value = 50.0
 norm_eps = 1e-06
+
+
+def tiled_gather(x, axis, dim):
+    copies = jnp.concatenate([x] * lax.axis_size(axis), axis=dim)
+    return lax.all_to_all(copies, axis, dim, dim, tiled=True)
 
 
 def from_behind(block, axis, distance):
@@ -114,7 +119,7 @@
     )
     placed = jnp.argsort(received[1])
     own_normed = received[0][placed]
-    group_normed = lax.all_gather(own_normed, "kv", axis=0, tiled=True)
+    group_normed = tiled_gather(own_normed, "kv", 0)
     own_stream = received[2][placed]
     resident_keys = received[3][placed]
     resident_values = received[4][placed]

time: 217 us -> 204 us (0.940)
  waiting for transfers between devices: 56.2 us -> 46.9 us
  blocking collectives: 4.22 us -> 9.99 us
  starting transfers between devices: 41.6 us -> 36 us
  matrix products: 48.9 us -> 45.5 us
    all_gather x1 -> x0, waiting for transfers between devices: 9.35 us -> none  [per_device(): group_normed = lax.all_gather(own_normed, 'kv', axis=0, tiled=True)]
    all_to_all x0 -> x1, blocking collectives: none -> 5.77 us  [tiled_gather(): return lax.all_to_all(copies, axis, dim, dim, tiled=True)]
    all_to_all x1, starting transfers between devices: 9.19 us -> 3.82 us  [send_rows(): lax.all_to_all(key_portion, ('req', 'kv'), split_axis=0, concat_axis=0, t...]
    dot_general x1, matrix products: 17.1 us -> 13.7 us  [per_device(): gate_part = jnp.dot(picked, gate_weight, preferred_element_type=jnp.float32)]
    unnamed x29 -> x27, local copies, waits for them, and re-layouts: 16.6 us -> 16.6 us
  transfers between devices with their start and end apart: 11 -> 10, of which waited for: 7 -> 6; matrix products, arithmetic and copies ran while one was open for 18% -> 19% of each run, Pallas kernels for 0% -> 0%
where the time goes in v1:
time: 204 us; the launch traced here: 203 us
  waiting for transfers between devices  46.9 us (23%)
  matrix products  45.5 us (22%)
  starting transfers between devices  36 us (18%)
  local copies, waits for them, and re-layouts  29.6 us (15%)
  other arithmetic  20.7 us (10%)
  between operations  14.4 us (7%)
  blocking collectives  9.99 us (5%)
    dot_general x1, matrix products, per_device(): jnp.dot(active, down_weight, preferred_element_type=jnp.float32)  24.6 us
    unnamed x27, local copies, waits for them, and re-layouts  16.6 us
    all_to_all x1, waiting for transfers between devices, send_rows(): lax.all_to_all(stream_part, ('req', 'kv'), split_axis=0, concat_axis=0, t...  14.5 us
    dot_general x1, matrix products, per_device(): gate_part = jnp.dot(picked, gate_weight, preferred_element_type=jnp.float32)  13.7 us
    all_to_all x1, waiting for transfers between devices, send_rows(): lax.all_to_all(normed_part, ('req', 'kv'), split_axis=0, concat_axis=0, t...  13 us
    all_to_all x1, starting transfers between devices, send_rows(): lax.all_to_all(normed_pos, ('req', 'kv'), split_axis=0, concat_axis=0, ti...  10.9 us
    all_to_all x1, waiting for transfers between devices, send_rows(): lax.all_to_all(key_portion, ('req', 'kv'), split_axis=0, concat_axis=0, t...  8.71 us
    all_to_all x1, starting transfers between devices, send_rows(): lax.all_to_all(normed_part, ('req', 'kv'), split_axis=0, concat_axis=0, t...  7.8 us
  transfers between devices with their start and end apart: 10, of which 6 were waited for; matrix products, arithmetic and copies ran while one was open for 19% of the time, Pallas kernels for 0%

profile of v1, /device:TPU:1, one launch (start us, length us, event | category | flops | bytes accessed | tf_op | source)
XLA Modules:
  0.0 203.2 jit_solution(10153086298071055397)
XLA Ops:
  7.9 1.3 collective-permute-start.1
  9.2 1.1 copy.46
  10.3 1.3 collective-permute-start.2
  11.6 1.3 collective-permute-start
  12.9 1.4 reshape.108
  14.5 1.0 collective-permute-done
  15.5 1.0 pad_maximum_fusion.1
  17.9 4.2 %all_to_all.88 = bf16[128,2,1024]{2,0,1:T(8,128)(2,1)S(1)} all-to-all(bf16[128,2,1024]{2,0,1:T(8,128)(2,1)S(1)} %copy.50), channel_id=1, replica_groups=mesh['req'=64,'kv'=2] {'kv'}, dimensions={1} | all-to-all | bytes 1048576 | tf_op jit(solution)/shard_map/all_to_all | solution.py:101
  22.1 6.4 %convolution_convert_fusion.1 = bf16[256,3584]{1,0:T(8,128)(2,1)} fusion(bf16[256,1024]{1,0:T(8,128)(2,1)S(1)} %bitcast.81, bf16[1024,3584]{1,0:T(8,128)(2,1)} %param.19), kind=kOutput, calls=%fused_computation.13 | convolution fusion | flops 1879965696 | bytes 9699328 | tf_op jit(solution)/shard_map/dot_general | solution.py:104
  29.2 2.5 %sort.31 = (s32[128]{0:T(128)}, s32[128]{0:T(128)S(1)}) sort(s32[128]{0:T(128)S(1)} %copy-done, s32[128]{0:T(128)S(1)} %iota.18), dimensions={0}, to_apply=%region_3.4 | sort | flops 896 | bytes 2048 | tf_op jit(solution)/shard_map/jit(argsort)/sort | solution.py:111
  31.8 1.2 gather_fusion.1
  33.8 10.9 %all-to-all-start.2 = ((s32[128,1,1]{2,1,0:T(1,128)}), s32[128,1,1]{2,1,0:T(1,128)S(1)}, u32[]{:S(2)}, u32[]{:S(2)}) async-start(s32[128,1,1]{2,1,0:T(1,128)} %copy.52), calls=%async_computation.3 | async-start | bytes 131072 | tf_op jit(solution)/shard_map/all_to_all | solution.py:54
  44.7 1.4 fusion.8
  46.2 1.8 fusion.12
  48.3 1.1 gather_fusion.3
  49.9 1.2 reduce.1
  51.1 1.1 reshape.195
  52.2 2.0 all-to-all-done.2
  54.2 7.8 %all-to-all-start.3 = ((bf16[128,2,1792]{2,1,0:T(2,128)(2,1)}), bf16[128,2,1792]{2,1,0:T(2,128)(2,1)S(1)}, u32[]{:S(2)}, u32[]{:S(2)}) async-start(bf16[128,2,1792]{2,1,0:T(2,128)(2,1)} %reshape.195), calls=%async_computation.4 | async-start | bytes 1835008 | tf_op jit(solution)/shard_map/all_to_all | solution.py:53
  62.0 2.4 %reduce = s32[128]{0:T(128)S(1)} reduce(s32[128,1,1]{2,1,0:T(1,128)S(1)} %all-to-all-done.2, s32[]{:T(128)} %constant.17.clone.1), dimensions={1,2}, to_apply=%all_to_all.67.reduce_sub_computation | reduce | bytes 1028 | tf_op jit(solution)/shard_map/all_to_all | solution.py:54
  64.4 2.5 %sort.32 = (s32[128]{0:T(128)}, s32[128]{0:T(128)S(1)}) sort(s32[128]{0:T(128)S(1)} %reduce, s32[128]{0:T(128)S(1)} %iota.19), dimensions={0}, to_apply=%region_4.5 | sort | flops 896 | bytes 2048 | tf_op jit(solution)/shard_map/jit(argsort)/sort | solution.py:120
  67.0 13.0 %all-to-all-done.3 = bf16[128,2,1792]{2,1,0:T(2,128)(2,1)S(1)} async-done(((bf16[128,2,1792]{2,1,0:T(2,128)(2,1)}), bf16[128,2,1792]{2,1,0:T(2,128)(2,1)S(1)}, u32[]{:S(2)}, u32[]{:S(2)}) %all-to-all-start.3) | async-done | bytes 917536 | tf_op jit(solution)/shard_map/all_to_all | solution.py:53
  79.9 2.1 %reshape.196 = bf16[128,1,3584]{2,1,0:T(2,128)(2,1)} reshape(bf16[128,2,1792]{2,1,0:T(2,128)(2,1)S(1)} %all-to-all-done.3) | data formatting | bytes 1835008
  82.0 1.6 copy.79
  83.7 1.1 gather_fusion.4
  84.9 5.8 %all_to_all.89 = bf16[2,128,3584]{2,1,0:T(8,128)(2,1)S(1)} all-to-all(bf16[2,128,3584]{2,1,0:T(8,128)(2,1)S(1)} %bitcast.69), channel_id=1, replica_groups=mesh['req'=64,'kv'=2] {'kv'}, dimensions={0} | all-to-all | bytes 3670016 | tf_op jit(solution)/shard_map/all_to_all | solution.py:16
  90.7 13.7 %fusion.43 = f32[256,3584]{1,0:T(8,128)} fusion(bf16[256,3584]{1,0:T(8,128)(2,1)S(1)} %bitcast.72, bf16[3584,3584]{1,0:T(8,128)(2,1)} %param.22), kind=kOutput, calls=%fused_computation.87 | convolution fusion | flops 6576668672 | bytes 31195136 | tf_op jit(solution)/shard_map/dot_general | solution.py:127
  104.4 24.6 %convolution_convert_fusion = bf16[256,3584]{1,0:T(8,128)(2,1)} fusion(bf16[3584,3584]{1,0:T(8,128)(2,1)} %param.24, bf16[256,3584]{1,0:T(8,128)(2,1)S(1)} %bitcast.73, bf16[3584,3584]{1,0:T(8,128)(2,1)} %param.23, f32[256,3584]{1,0:T(8,128)} %fusion.43), kind=kOutput, calls=%fused_computation.12 | convolution fusion | flops 13163429888 | bytes 58720256 | tf_op jit(solution)/shard_map/dot_general | solution.py:131
  129.0 0.9 copy-done.1
  129.9 0.9 gather_fusion.5
  131.4 0.9 reshape.199
  132.3 3.8 %all-to-all-start.5 = ((bf16[128,2,512]{2,1,0:T(2,128)(2,1)}), bf16[128,2,512]{2,1,0:T(2,128)(2,1)S(1)}, u32[]{:S(2)}, u32[]{:S(2)}) async-start(bf16[128,2,512]{2,1,0:T(2,128)(2,1)} %reshape.199), calls=%async_computation.7 | async-start | bytes 524288 | tf_op jit(solution)/shard_map/all_to_all | solution.py:56
  136.1 0.9 gather_fusion.7
  137.7 0.9 reshape.201
  138.6 8.7 %all-to-all-done.5 = bf16[128,2,512]{2,1,0:T(2,128)(2,1)S(1)} async-done(((bf16[128,2,512]{2,1,0:T(2,128)(2,1)}), bf16[128,2,512]{2,1,0:T(2,128)(2,1)S(1)}, u32[]{:S(2)}, u32[]{:S(2)}) %all-to-all-start.5) | async-done | bytes 262176 | tf_op jit(solution)/shard_map/all_to_all | solution.py:56
  147.3 4.4 %all-to-all-start.6 = ((bf16[128,2,512]{2,1,0:T(2,128)(2,1)}), bf16[128,2,512]{2,1,0:T(2,128)(2,1)S(1)}, u32[]{:S(2)}, u32[]{:S(2)}) async-start(bf16[128,2,512]{2,1,0:T(2,128)(2,1)} %reshape.201), calls=%async_computation.8 | async-start | bytes 524288 | tf_op jit(solution)/shard_map/all_to_all | solution.py:57
  151.7 1.1 gather_fusion
  152.8 1.2 reduce.2
  154.1 1.1 reshape.197
  155.2 7.6 %all-to-all-done.6 = bf16[128,2,512]{2,1,0:T(2,128)(2,1)S(1)} async-done(((bf16[128,2,512]{2,1,0:T(2,128)(2,1)}), bf16[128,2,512]{2,1,0:T(2,128)(2,1)S(1)}, u32[]{:S(2)}, u32[]{:S(2)}) %all-to-all-start.6) | async-done | bytes 262176 | tf_op jit(solution)/shard_map/all_to_all | solution.py:57
  162.8 5.1 %all-to-all-start.1 = ((bf16[128,2,1792]{2,1,0:T(2,128)(2,1)}), bf16[128,2,1792]{2,1,0:T(2,128)(2,1)}, u32[]{:S(2)}, u32[]{:S(2)}) async-start(bf16[128,2,1792]{2,1,0:T(2,128)(2,1)} %reshape.197), calls=%async_computation.2 | async-start | bytes 1835008 | tf_op jit(solution)/shard_map/all_to_all | solution.py:55
  168.3 0.9 gather_fusion.6
  169.5 0.9 gather_fusion.8
  171.2 14.5 %all-to-all-done.1 = bf16[128,2,1792]{2,1,0:T(2,128)(2,1)} async-done(((bf16[128,2,1792]{2,1,0:T(2,128)(2,1)}), bf16[128,2,1792]{2,1,0:T(2,128)(2,1)}, u32[]{:S(2)}, u32[]{:S(2)}) %all-to-all-start.1) | async-done | bytes 917536 | tf_op jit(solution)/shard_map/all_to_all | solution.py:55
  185.7 5.4 %reshape.198 = bf16[128,1,3584]{2,1,0:T(2,128)(2,1)S(1)} reshape(bf16[128,2,1792]{2,1,0:T(2,128)(2,1)} %all-to-all-done.1) | data formatting | bytes 1835008
  191.2 1.1 gather_fusion.2
  192.4 1.4 fusion.15
  193.9 2.5 %fusion.18 = bf16[128,3584]{1,0:T(8,128)(2,1)} fusion(bf16[128,3584]{1,0:T(8,128)(2,1)} %reduce-scatter.5.cloned.1.call-done, bf16[128,3584]{1,0:T(8,128)(2,1)S(1)} %gather_fusion.2, f32[3584]{0:T(1024)S(1)} %copy-done.6, f32[128]{0:T(128)S(1)} %add_rsqrt_fusion), kind=kLoop, calls=%fused_computation.37 | loop fusion | flops 2752512 | bytes 2767360 | tf_op jit(solution)/shard_map/convert_element_type | solution.py:136
  (54 shorter events, 7.6 us)
Async XLA Ops:
  7.2 37.5 %reduce-scatter.3.cloned.1.call-start = ((), (), s32[]{:S(2)}) async-start(), calls=%async_computation.9 | async-start | bytes 2752512 | tf_op jit(solution)/shard_map/reduce_scatter | solution.py:103
  7.9 6.5 %collective-permute-start.1 = (s32[128]{0:T(128)S(1)}, s32[128]{0:T(128)S(1)}, u32[]{:S(2)}, u32[]{:S(2)}) collective-permute-start(s32[128]{0:T(128)S(1)} %broadcast_add_fusion), channel_id=1, source_target_pairs={{0,1},{2,3},{4,5},{6,7},{8,9},{10,11},{12,13},{14,15},{16,17},{18,... | collective-permute-start | bytes 1544 | tf_op jit(solution)/shard_map/ppermute | solution.py:22
  10.3 6.4 %collective-permute-start.2 = (bf16[128,1024]{0,1:T(8,128)(2,1)S(1)}, bf16[128,1024]{0,1:T(8,128)(2,1)S(1)}, u32[]{:S(2)}, u32[]{:S(2)}) collective-permute-start(bf16[128,1024]{0,1:T(8,128)(2,1)S(1)} %copy.46), channel_id=1, source_target_pairs={{0,1},{2,3},{4,5},{6,7},{8,9},{10,11},{12,13},{14,15},{16,17},{18,... | collective-permute-start | bytes 786440 | tf_op jit(solution)/shard_map/ppermute | solution.py:22
  11.6 4.0 %collective-permute-start = (bf16[128,1024]{1,0:T(8,128)(2,1)}, bf16[128,1024]{1,0:T(8,128)(2,1)S(1)}, u32[]{:S(2)}, u32[]{:S(2)}) collective-permute-start(bf16[128,1024]{1,0:T(8,128)(2,1)} %param.15), channel_id=1, source_target_pairs={{0,1},{2,3},{4,5},{6,7},{8,9},{10,11},{12,13},{14,15},{16,17},{18,... | collective-permute-start | bytes 786440 | tf_op jit(solution)/shard_map/ppermute | solution.py:22
  28.6 0.7 copy-start
  28.6 17.6 %copy-start.3 = (bf16[128,3584]{1,0:T(8,128)(2,1)S(1)}, bf16[128,3584]{1,0:T(8,128)(2,1)}, u32[]{:S(2)}) copy-start(bf16[128,3584]{1,0:T(8,128)(2,1)} %param.16) | copy-start | bytes 2752516
  28.6 17.6 %copy-start.4 = (f32[3584]{0:T(1024)S(1)}, f32[3584]{0:T(1024)}, u32[]{:S(2)}) copy-start(f32[3584]{0:T(1024)} %param.20) | copy-start | bytes 43012
  33.8 20.4 %all-to-all-start.2 = ((s32[128,1,1]{2,1,0:T(1,128)}), s32[128,1,1]{2,1,0:T(1,128)S(1)}, u32[]{:S(2)}, u32[]{:S(2)}) async-start(s32[128,1,1]{2,1,0:T(1,128)} %copy.52), calls=%async_computation.3 | async-start | bytes 131072 | tf_op jit(solution)/shard_map/all_to_all | solution.py:54
  44.7 3.3 %copy-start.5 = (f32[3584]{0:T(1024)S(1)}, f32[3584]{0:T(1024)}, u32[]{:S(2)}) copy-start(f32[3584]{0:T(1024)} %param.21) | copy-start | bytes 43012
  54.2 25.8 %all-to-all-start.3 = ((bf16[128,2,1792]{2,1,0:T(2,128)(2,1)}), bf16[128,2,1792]{2,1,0:T(2,128)(2,1)S(1)}, u32[]{:S(2)}, u32[]{:S(2)}) async-start(bf16[128,2,1792]{2,1,0:T(2,128)(2,1)} %reshape.195), calls=%async_computation.4 | async-start | bytes 1835008 | tf_op jit(solution)/shard_map/all_to_all | solution.py:53
  62.0 130.4 %reduce-scatter.5.cloned.1.call-start = ((), (), s32[]{:S(2)}) async-start(), calls=%async_computation.10 | async-start | bytes 2752512 | tf_op jit(solution)/shard_map/reduce_scatter | solution.py:130
  128.9 0.9 copy-start.1
  129.9 6.3 %copy-start.2 = (bf16[128,1024]{1,0:T(8,128)(2,1)S(1)}, bf16[128,1024]{1,0:T(8,128)(2,1)}, u32[]{:S(2)}) copy-start(bf16[128,1024]{1,0:T(8,128)(2,1)} %param.15) | copy-start | bytes 786436
  132.3 15.0 %all-to-all-start.5 = ((bf16[128,2,512]{2,1,0:T(2,128)(2,1)}), bf16[128,2,512]{2,1,0:T(2,128)(2,1)S(1)}, u32[]{:S(2)}, u32[]{:S(2)}) async-start(bf16[128,2,512]{2,1,0:T(2,128)(2,1)} %reshape.199), calls=%async_computation.7 | async-start | bytes 524288 | tf_op jit(solution)/shard_map/all_to_all | solution.py:56
  147.3 15.5 %all-to-all-start.6 = ((bf16[128,2,512]{2,1,0:T(2,128)(2,1)}), bf16[128,2,512]{2,1,0:T(2,128)(2,1)S(1)}, u32[]{:S(2)}, u32[]{:S(2)}) async-start(bf16[128,2,512]{2,1,0:T(2,128)(2,1)} %reshape.201), calls=%async_computation.8 | async-start | bytes 524288 | tf_op jit(solution)/shard_map/all_to_all | solution.py:57
  162.8 22.9 %all-to-all-start.1 = ((bf16[128,2,1792]{2,1,0:T(2,128)(2,1)}), bf16[128,2,1792]{2,1,0:T(2,128)(2,1)}, u32[]{:S(2)}, u32[]{:S(2)}) async-start(bf16[128,2,1792]{2,1,0:T(2,128)(2,1)} %reshape.197), calls=%async_computation.2 | async-start | bytes 1835008 | tf_op jit(solution)/shard_map/all_to_all | solution.py:55
  191.2 2.6 %copy-start.6 = (f32[3584]{0:T(1024)S(1)}, f32[3584]{0:T(1024)}, u32[]{:S(2)}) copy-start(f32[3584]{0:T(1024)} %param.25) | copy-start | bytes 43012
Sparse Core Ops, SparseCore 0:
  28.7 15.0 reduce-scatter.2
  129.1 7.9 reduce-scatter.4
